TPU v7x, 32 devices: a whole 2x2x4 slice. The times are simulated.
32 devices in a mesh: tile: 8 (over z, y), src: 4 (over x, core).
Axes of the slice: x: 2, y: 2, z: 4, core: 2. Of those that a mesh axis runs over, the one named last changes fastest.
Arguments:
- excitation: bfloat16 [2, 512, 8192], P(None, 'src', 'tile'), may hold values from -6 to 6
- near_blocks: bfloat16 [16, 3, 2, 512, 512], P('tile'), may hold values from -0.02734375 to 0.02734375
- source_basis: bfloat16 [16, 2, 24, 512], P('tile'), may hold values from -0.1875 to 0.1875
- target_basis: bfloat16 [16, 2, 24, 512], P('tile'), may hold values from -0.625 to 0.625
- coupling: bfloat16 [2, 384, 384], P(None, None, 'tile'), may hold values from -0.109375 to 0.109375
- pair_rank: int32 [16, 16], P(None, 'tile'), may hold values from 2 to 24
- far_link: int32 [16, 16], P(None, 'tile'), may hold values 0 or 1
- focal_kernel: bfloat16 [2, 64, 8192], P(None, None, 'tile'), may hold values from -0.046875 to 0.046875
- focal_target: float32 [64], replicated, may hold values from 0.3 to 0.9
- focal_owner: int32 [64], replicated, may hold values from 0 to 63, each once
Outputs:
- field: float32 [2, 512, 8192], P(None, 'src', 'tile')
- focal_residual: float32 [64], P('tile')
- adjoint: float32 [2, 512, 8192], P(None, 'src', 'tile')
Inputs may be any that keep to these rules, and one draw needn't show every extreme that they name: `focal_owner`: each focal point has its own slot; slot k belongs to index k // 8 of tile.
All inputs are finite; a program needn't handle non-finite values. No bound on the sum of `far_link` on one device may be relied on, other than what follows from the above.
Results may differ from a plain program's by a relative error of at most 0.006.
Values may be sent and summed in bfloat16 or wider, within the bound.
No kernel may reach another device: no remote copies, remote signals or barrier semaphores. Data moves between devices by JAX's collectives and lax.ppermute only.
A program may use at most 64 MiB of HBM per device.

v0:
```python
import jax
import jax.numpy as jnp
from jax import lax
from jax.sharding import PartitionSpec as P

TILE = 512
RANK = 24
DAMPING = 0.8


def extended(x, sides, width):
    for axis, dim in sides:
        size, length = (lax.axis_size(axis), x.shape[dim])
        up = [(i, (i + 1) % size) for i in range(size)]
        down = [(j, i) for i, j in up]
        last = lax.slice_in_dim(x, length - width, length, axis=dim)
        initial = lax.slice_in_dim(x, 0, width, axis=dim)
        before = lax.ppermute(last, axis, up)
        after = lax.ppermute(initial, axis, down)
        x = jnp.concatenate([before, x, after], axis=dim)
    return x


def plain_dot(left, right, contract):
    return lax.dot_general(
        left, right, (((1,), (contract,)), ((), ())), preferred_element_type=jnp.float32
    )


def complex_dot(left_re, left_im, right_re, right_im, contract):
    real_part = plain_dot(left_re, right_re, contract) - plain_dot(left_im, right_im, contract)
    imag_part = plain_dot(left_re, right_im, contract) + plain_dot(left_im, right_re, contract)
    return (real_part, imag_part)


def per_device(
    excitation,
    near_blocks,
    source_basis,
    target_basis,
    coupling,
    pair_rank,
    far_link,
    focal_kernel,
    focal_target,
    focal_owner,
):
    tile_count = near_blocks.shape[0]
    src_rows = excitation.shape[1]
    tiles = pair_rank.shape[0]
    focal_count = focal_target.shape[0]
    first_tile = lax.axis_index("tile") * tile_count
    global_tiles = first_tile + jnp.arange(tile_count)
    source_tiles = jnp.arange(tiles)[:, None]
    distance = (global_tiles[None, :] - source_tiles) % tiles
    far_pairs = (far_link == 1) & (distance != 0) & (distance != 1) & (distance != tiles - 1)
    levels = jnp.arange(RANK)
    rank_limit = pair_rank[:, None, :, None]
    rank_mask = (
        far_pairs[:, None, :, None]
        & (levels[None, :, None, None] < rank_limit)
        & (levels[None, None, None, :] < rank_limit)
    )
    rank_mask = rank_mask.reshape(tiles * RANK, tile_count * RANK)
    masked = coupling * rank_mask.astype(coupling.dtype)
    flipped = lax.all_to_all(masked, "tile", split_axis=1, concat_axis=2, tiled=True)

    def apply_transpose(field):
        field_bf = field.astype(jnp.bfloat16)
        moved_re = [[], [], []]
        moved_im = [[], [], []]
        proj_re = []
        proj_im = []
        for tile_here in range(tile_count):
            own = field_bf[:, :, tile_here * TILE : (tile_here + 1) * TILE]
            for offset in range(3):
                part_re, part_im = complex_dot(
                    own[0],
                    own[1],
                    near_blocks[tile_here, offset, 0],
                    near_blocks[tile_here, offset, 1],
                    1,
                )
                moved_re[offset].append(part_re)
                moved_im[offset].append(part_im)
            part_re, part_im = complex_dot(
                own[0], own[1], target_basis[tile_here, 0], target_basis[tile_here, 1], 1
            )
            proj_re.append(part_re)
            proj_im.append(part_im)
        moved = [
            jnp.stack([jnp.concatenate(moved_re[k], axis=1), jnp.concatenate(moved_im[k], axis=1)])
            for k in range(3)
        ]
        width = tile_count * TILE
        edges = jnp.concatenate([moved[0][:, :, 0:TILE], moved[2][:, :, width - TILE :]], axis=2)
        arrived = extended(edges.astype(jnp.bfloat16), (("tile", 2),), TILE).astype(edges.dtype)
        from_left = jnp.concatenate(
            [arrived[:, :, 0:TILE], moved[2][:, :, 0 : width - TILE]], axis=2
        )
        from_right = jnp.concatenate(
            [moved[0][:, :, TILE:], arrived[:, :, 3 * TILE : 4 * TILE]], axis=2
        )
        near_part = moved[1] + from_left + from_right
        projected = jnp.stack(
            [jnp.concatenate(proj_re, axis=1), jnp.concatenate(proj_im, axis=1)]
        ).astype(jnp.bfloat16)
        shard_piece = lax.all_gather(projected, "tile", axis=2, tiled=True)
        term_re, term_im = complex_dot(shard_piece[0], shard_piece[1], flipped[0], flipped[1], 1)
        summed_back = jnp.stack([term_re, term_im]).astype(jnp.bfloat16)
        far_re = []
        far_im = []
        for tile_here in range(tile_count):
            piece = summed_back[:, :, tile_here * RANK : (tile_here + 1) * RANK]
            part_re, part_im = complex_dot(
                piece[0], piece[1], source_basis[tile_here, 0], source_basis[tile_here, 1], 0
            )
            far_re.append(part_re)
            far_im.append(part_im)
        far_part = jnp.stack([jnp.concatenate(far_re, axis=1), jnp.concatenate(far_im, axis=1)])
        return field + near_part + far_part

    right_side = excitation.astype(jnp.float32)
    field = right_side
    for update in range(2):
        apply_field_bf = field.astype(jnp.bfloat16)
        padded = extended(apply_field_bf, (("tile", 2),), TILE)
        coeff_re = []
        coeff_im = []
        for apply_tile_here in range(tile_count):
            apply_own = apply_field_bf[:, :, apply_tile_here * TILE : (apply_tile_here + 1) * TILE]
            apply_part_re, apply_part_im = complex_dot(
                apply_own[0],
                apply_own[1],
                source_basis[apply_tile_here, 0],
                source_basis[apply_tile_here, 1],
                1,
            )
            coeff_re.append(apply_part_re)
            coeff_im.append(apply_part_im)
        coeff = jnp.stack(
            [jnp.concatenate(coeff_re, axis=1), jnp.concatenate(coeff_im, axis=1)]
        ).astype(jnp.bfloat16)
        fold_shard_piece = lax.all_gather(coeff, "tile", axis=2, tiled=True)
        fold_term_re, fold_term_im = complex_dot(
            fold_shard_piece[0], fold_shard_piece[1], masked[0], masked[1], 0
        )
        coupled = jnp.stack([fold_term_re, fold_term_im]).astype(jnp.bfloat16)
        out_re = []
        out_im = []
        for apply_tile_here in range(tile_count):
            total_re = jnp.zeros((src_rows, TILE), jnp.float32)
            total_im = jnp.zeros((src_rows, TILE), jnp.float32)
            for apply_offset in range(3):
                window = padded[
                    :,
                    :,
                    (apply_tile_here + apply_offset)
                    * TILE : (apply_tile_here + apply_offset + 1)
                    * TILE,
                ]
                apply_part_re, apply_part_im = complex_dot(
                    window[0],
                    window[1],
                    near_blocks[apply_tile_here, apply_offset, 0],
                    near_blocks[apply_tile_here, apply_offset, 1],
                    0,
                )
                total_re = total_re + apply_part_re
                total_im = total_im + apply_part_im
            apply_piece = coupled[:, :, apply_tile_here * RANK : (apply_tile_here + 1) * RANK]
            apply_part_re, apply_part_im = complex_dot(
                apply_piece[0],
                apply_piece[1],
                target_basis[apply_tile_here, 0],
                target_basis[apply_tile_here, 1],
                0,
            )
            out_re.append(total_re + apply_part_re)
            out_im.append(total_im + apply_part_im)
        added = jnp.stack([jnp.concatenate(out_re, axis=1), jnp.concatenate(out_im, axis=1)])
        field = field + DAMPING * (right_side - (field + added))
    field_bf = field.astype(jnp.bfloat16)
    focal_re, focal_im = complex_dot(field_bf[0], field_bf[1], focal_kernel[0], focal_kernel[1], 1)
    slots_here = focal_count // lax.axis_size("tile")
    first_slot = lax.axis_index("tile") * slots_here
    sources = src_rows * lax.axis_size("src")
    permute = (focal_owner[:, None] == jnp.arange(focal_count)[None, :]).astype(jnp.float32)
    summed_focal = lax.psum(jnp.stack([focal_re, focal_im]), "tile")
    intensity = lax.psum(
        jnp.sum(summed_focal[0] * summed_focal[0] + summed_focal[1] * summed_focal[1], axis=0),
        "src",
    )
    residual_part = jnp.tanh(intensity / (2.0 * sources)) - focal_target
    weights_re = (residual_part * summed_focal[0]).astype(jnp.bfloat16)
    weights_im = (-residual_part * summed_focal[1]).astype(jnp.bfloat16)
    residual_slots = jnp.dot(residual_part, permute, precision=lax.Precision.HIGHEST)
    residual_out = lax.dynamic_slice_in_dim(residual_slots, first_slot, slots_here)
    scale_factor = (tiles * TILE / focal_count) ** 0.5
    term_re, term_im = complex_dot(weights_re, weights_im, focal_kernel[0], focal_kernel[1], 0)
    source_term = jnp.stack([term_re, term_im]) * scale_factor
    adjoint = source_term + DAMPING * (source_term - apply_transpose(source_term))
    return (field, residual_out, adjoint)


def solution(mesh):
    return jax.shard_map(
        per_device,
        mesh=mesh,
        in_specs=(
            P(None, "src", "tile"),
            P("tile", None, None, None, None),
            P("tile", None, None, None),
            P("tile", None, None, None),
            P(None, None, "tile"),
            P(None, "tile"),
            P(None, "tile"),
            P(None, None, "tile"),
            P(),
            P(),
        ),
        out_specs=(P(None, "src", "tile"), P("tile"), P(None, "src", "tile")),
        check_vma=False,
    )
```

profile of v0, /device:TPU:0, one launch (start us, length us, event | category | flops | bytes accessed | tf_op | source)
XLA Modules:
  0.0 293.0 jit_solution(17563514672564382302)
XLA Ops:
  7.2 2.0 fusion.459
  9.1 6.0 %collective-permute-start.1 = (bf16[2,128,512]{2,1,0:T(8,128)(2,1)}, bf16[2,128,512]{2,1,0:T(8,128)(2,1)}, u32[]{:S(2)}, u32[]{:S(2)}) collective-permute-start(bf16[2,128,512]{2,1,0:T(8,128)(2,1)} %get-tuple-element.12), channel_id=1, source_target_pairs={{4,0},{8,4},{12,8},{16,12},{20,16},{24,20},{28,24},{0,28},{5,1},{9... | collective-permute-start | bytes 786440 | tf_op jit(solution)/shard_map/ppermute | solution.py:19
  19.8 6.0 %all-to-all-start = ((bf16[8,2,2304]{2,1,0:T(2,128)(2,1)}), bf16[8,2,2304]{2,1,0:T(2,128)(2,1)S(1)}, u32[]{:S(2)}, u32[]{:S(2)}) async-start(bf16[8,2,2304]{2,1,0:T(2,128)(2,1)} %reshape.84), calls=%async_computation | async-start | bytes 147456 | tf_op jit(solution)/shard_map/all_to_all | solution.py:66
  25.8 1.2 fusion.274
  27.0 1.3 fusion.288
  28.4 1.1 fusion.272
  29.4 1.1 fusion.286
  30.5 1.1 fusion.41
  31.5 1.1 fusion.40
  32.6 1.1 fusion.43
  33.7 1.1 fusion.42
  34.8 31.3 %all_gather.9 = bf16[2,128,384]{1,2,0:T(8,128)(2,1)S(1)} all-gather(bf16[2,128,48]{1,2,0:T(8,128)(2,1)S(1)} %pad_maximum_fusion.6), channel_id=1, replica_groups=mesh['tile'=8,'src'=4] {'tile'}, dimensions={2}, use_global_device_ids=true | all-gather | bytes 221184 | tf_op jit(solution)/shard_map/all_gather | solution.py:144
  66.3 1.3 fusion.94
  67.7 1.3 fusion.112
  69.6 1.3 fusion.130
  70.9 1.3 fusion.148
  74.9 1.0 convolution_add_fusion.16
  78.9 0.9 convolution_subtract_fusion.17
  79.8 0.9 fusion.6
  80.8 0.9 fusion.3
  83.1 1.2 copy.22
  84.3 1.8 fusion.85
  86.1 1.3 fusion.175
  87.4 1.5 fusion.20
  88.9 1.5 fusion.22
  90.5 1.3 fusion.77
  91.8 1.1 fusion.167
  93.0 1.1 fusion.23
  94.2 1.2 fusion.25
  96.9 30.7 %all_gather.10 = bf16[2,128,384]{1,2,0:T(8,128)(2,1)S(1)} all-gather(bf16[2,128,48]{1,2,0:T(8,128)(2,1)S(1)} %pad_maximum_fusion.7), channel_id=1, replica_groups=mesh['tile'=8,'src'=4] {'tile'}, dimensions={2}, use_global_device_ids=true | all-gather | bytes 221184 | tf_op jit(solution)/shard_map/all_gather | solution.py:144
  131.0 4.0 %collective-permute-start.3 = (bf16[2,128,512]{2,1,0:T(8,128)(2,1)S(1)}, bf16[2,128,512]{2,1,0:T(8,128)(2,1)S(1)}, u32[]{:S(2)}, u32[]{:S(2)}) collective-permute-start(bf16[2,128,512]{2,1,0:T(8,128)(2,1)S(1)} %get-tuple-element.10), channel_id=1, source_target_pairs={{4,0},{8,4},{12,8},{16,12},{20,16},{24,20},{28,24},{0,28},{5,1},{9... | collective-permute-start | bytes 786440 | tf_op jit(solution)/shard_map/ppermute | solution.py:19
  137.9 1.1 collective-permute-done.3
  139.2 5.9 %collective-permute-done.2 = bf16[2,128,512]{2,1,0:T(8,128)(2,1)S(1)} collective-permute-done((bf16[2,128,512]{2,1,0:T(8,128)(2,1)S(1)}, bf16[2,128,512]{2,1,0:T(8,128)(2,1)S(1)}, u32[]{:S(2)}, u32[]{:S(2)}) %collective-permute-start.2) | collective-permute-done | bytes 262176 | tf_op jit(solution)/shard_map/ppermute | solution.py:18
  147.0 1.3 fusion.456
  150.1 66.4 %all-reduce.2.cloned.1.call-done = f32[2,128,64]{1,2,0:T(8,128)} async-done(((f32[2,128,64]{1,2,0:T(8,128)}), f32[2,128,64]{1,2,0:T(8,128)}) %all-reduce.2.cloned.1.call-update) | async-done | bytes 65552 | tf_op jit(solution)/shard_map/psum | solution.py:189
  217.4 5.8 %psum.15 = f32[64]{0:T(128)S(1)} all-reduce(f32[64]{0:T(128)S(1)} %add_reduce_fusion), channel_id=1, replica_groups=mesh['tile'=8,'src'=4] {'src'}, use_global_device_ids=true, to_apply=%region_2.3 | all-reduce | flops 64 | bytes 512 | tf_op jit(solution)/shard_map/psum | solution.py:190
  223.2 1.2 fusion.253
  224.5 1.1 fusion.259
  225.6 1.1 fusion
  226.7 1.1 fusion.1
  227.9 1.3 fusion.106
  229.2 1.4 fusion.160
  230.6 1.3 fusion.116
  236.1 30.7 %all_gather.11 = bf16[2,128,384]{1,2,0:T(8,128)(2,1)S(1)} all-gather(bf16[2,128,48]{1,2,0:T(8,128)(2,1)S(1)} %pad_maximum_fusion.8), channel_id=1, replica_groups=mesh['tile'=8,'src'=4] {'tile'}, dimensions={2}, use_global_device_ids=true | all-gather | bytes 221184 | tf_op jit(solution)/shard_map/all_gather | solution.py:108
  272.0 3.3 %collective-permute-start.5 = (bf16[2,128,512]{2,1,0:T(8,128)(2,1)S(1)}, bf16[2,128,512]{2,1,0:T(8,128)(2,1)S(1)}, u32[]{:S(2)}, u32[]{:S(2)}) collective-permute-start(bf16[2,128,512]{2,1,0:T(8,128)(2,1)S(1)} %fusion.67), channel_id=1, source_target_pairs={{4,0},{8,4},{12,8},{16,12},{20,16},{24,20},{28,24},{0,28},{5,1},{9... | collective-permute-start | bytes 786440 | tf_op jit(solution)/shard_map/ppermute | solution.py:19
  277.4 2.2 collective-permute-done.5
  279.7 4.8 %collective-permute-done.4 = bf16[2,128,512]{2,1,0:T(8,128)(2,1)S(1)} collective-permute-done((bf16[2,128,512]{2,1,0:T(8,128)(2,1)S(1)}, bf16[2,128,512]{2,1,0:T(8,128)(2,1)S(1)}, u32[]{:S(2)}, u32[]{:S(2)}) %collective-permute-start.4) | collective-permute-done | bytes 262176 | tf_op jit(solution)/shard_map/ppermute | solution.py:18
  284.6 1.6 fusion.61
  (195 shorter events, 36.0 us)
Async XLA Ops:
  7.2 62.5 %copy-start.1 = (bf16[2,128,1024]{2,1,0:T(8,128)(2,1)S(1)}, bf16[2,128,1024]{2,1,0:T(8,128)(2,1)}, u32[]{:S(2)}) copy-start(bf16[2,128,1024]{2,1,0:T(8,128)(2,1)} %param.10) | copy-start | bytes 1572868
  7.2 62.0 %copy-start.2 = (bf16[2,2,24,512]{3,2,1,0:T(8,128)(2,1)S(1)}, bf16[2,2,24,512]{3,2,1,0:T(8,128)(2,1)}, u32[]{:S(2)}) copy-start(bf16[2,2,24,512]{3,2,1,0:T(8,128)(2,1)} %param.13) | copy-start | bytes 294916
  9.1 75.1 %collective-permute-start.1 = (bf16[2,128,512]{2,1,0:T(8,128)(2,1)}, bf16[2,128,512]{2,1,0:T(8,128)(2,1)}, u32[]{:S(2)}, u32[]{:S(2)}) collective-permute-start(bf16[2,128,512]{2,1,0:T(8,128)(2,1)} %get-tuple-element.12), channel_id=1, source_target_pairs={{4,0},{8,4},{12,8},{16,12},{20,16},{24,20},{28,24},{0,28},{5,1},{9... | collective-permute-start | bytes 786440 | tf_op jit(solution)/shard_map/ppermute | solution.py:19
  15.2 70.9 %collective-permute-start = (bf16[2,128,512]{2,1,0:T(8,128)(2,1)}, bf16[2,128,512]{2,1,0:T(8,128)(2,1)}, u32[]{:S(2)}, u32[]{:S(2)}) collective-permute-start(bf16[2,128,512]{2,1,0:T(8,128)(2,1)} %get-tuple-element.11), channel_id=1, source_target_pairs={{0,4},{4,8},{8,12},{12,16},{16,20},{20,24},{24,28},{28,0},{1,5},{5... | collective-permute-start | bytes 786440 | tf_op jit(solution)/shard_map/ppermute | solution.py:18
  19.8 62.4 %all-to-all-start = ((bf16[8,2,2304]{2,1,0:T(2,128)(2,1)}), bf16[8,2,2304]{2,1,0:T(2,128)(2,1)S(1)}, u32[]{:S(2)}, u32[]{:S(2)}) async-start(bf16[8,2,2304]{2,1,0:T(2,128)(2,1)} %reshape.84), calls=%async_computation | async-start | bytes 147456 | tf_op jit(solution)/shard_map/all_to_all | solution.py:66
  25.8 190.7 %all-reduce.2.cloned.1.call-start = ((), (), s32[]{:S(2)}) async-start(), calls=%async_computation.1 | async-start | bytes 131072 | tf_op jit(solution)/shard_map/psum | solution.py:189
  25.8 46.6 %copy-start = (bf16[2,3,2,512,512]{4,3,2,1,0:T(8,128)(2,1)S(1)}, bf16[2,3,2,512,512]{4,3,2,1,0:T(8,128)(2,1)}, u32[]{:S(2)}) copy-start(bf16[2,3,2,512,512]{4,3,2,1,0:T(8,128)(2,1)} %param.11) | copy-start | bytes 18874372
  77.7 14.1 %slice-start = ((s8[6291456]{0:T(1024)(128)(4,1)}), s8[2097152]{0:T(1024)(128)(4,1)S(1)}, s32[]{:S(2)}) async-start(s8[6291456]{0:T(1024)(128)(4,1)} %bitcast.613), calls=%async_computation.2 | async-start | bytes 4194304
  83.1 9.9 %copy-start.6 = (f32[128,512]{1,0:T(8,128)S(1)}, f32[128,512]{1,0:T(8,128)}, u32[]{:S(2)}) copy-start(f32[128,512]{1,0:T(8,128)} %convolution_subtract_fusion.23) | copy-start | bytes 786436
  83.1 9.9 %copy-start.7 = (f32[128,512]{1,0:T(8,128)S(1)}, f32[128,512]{1,0:T(8,128)}, u32[]{:S(2)}) copy-start(f32[128,512]{1,0:T(8,128)} %fusion.3) | copy-start | bytes 786436
  83.1 11.1 %copy-start.4 = (f32[128,512]{1,0:T(8,128)S(1)}, f32[128,512]{1,0:T(8,128)}, u32[]{:S(2)}) copy-start(f32[128,512]{1,0:T(8,128)} %convolution_subtract_fusion.16) | copy-start | bytes 786436
  83.1 11.1 %copy-start.5 = (f32[128,512]{1,0:T(8,128)S(1)}, f32[128,512]{1,0:T(8,128)}, u32[]{:S(2)}) copy-start(f32[128,512]{1,0:T(8,128)} %convolution_subtract_fusion.17) | copy-start | bytes 786436
  83.1 8.8 %slice-start.1 = ((s8[6291456]{0:T(1024)(128)(4,1)}), s8[4194304]{0:T(1024)(128)(4,1)S(1)}, s32[]{:S(2)}) async-start(s8[6291456]{0:T(1024)(128)(4,1)} %bitcast.613), calls=%async_computation.3 | async-start | bytes 8388608
  87.4 8.2 %copy-start.8 = (bf16[2,2,24,512]{3,2,1,0:T(8,128)(2,1)S(1)}, bf16[2,2,24,512]{3,2,1,0:T(8,128)(2,1)}, u32[]{:S(2)}) copy-start(bf16[2,2,24,512]{3,2,1,0:T(8,128)(2,1)} %param.12) | copy-start | bytes 294916
  131.0 7.9 %collective-permute-start.3 = (bf16[2,128,512]{2,1,0:T(8,128)(2,1)S(1)}, bf16[2,128,512]{2,1,0:T(8,128)(2,1)S(1)}, u32[]{:S(2)}, u32[]{:S(2)}) collective-permute-start(bf16[2,128,512]{2,1,0:T(8,128)(2,1)S(1)} %get-tuple-element.10), channel_id=1, source_target_pairs={{4,0},{8,4},{12,8},{16,12},{20,16},{24,20},{28,24},{0,28},{5,1},{9... | collective-permute-start | bytes 786440 | tf_op jit(solution)/shard_map/ppermute | solution.py:19
  136.0 9.1 %collective-permute-start.2 = (bf16[2,128,512]{2,1,0:T(8,128)(2,1)S(1)}, bf16[2,128,512]{2,1,0:T(8,128)(2,1)S(1)}, u32[]{:S(2)}, u32[]{:S(2)}) collective-permute-start(bf16[2,128,512]{2,1,0:T(8,128)(2,1)S(1)} %get-tuple-element.9), channel_id=1, source_target_pairs={{0,4},{4,8},{8,12},{12,16},{16,20},{20,24},{24,28},{28,0},{1,5},{5... | collective-permute-start | bytes 786440 | tf_op jit(solution)/shard_map/ppermute | solution.py:18
  145.9 2.4 copy-start.3
  146.2 77.1 %copy-start.10 = (f32[64]{0:T(128)S(1)}, f32[64]{0:T(128)}, u32[]{:S(2)}) copy-start(f32[64]{0:T(128)} %param.18) | copy-start | bytes 772
  147.0 85.0 %slice-start.2 = ((s8[6291456]{0:T(1024)(128)(4,1)}), s8[2097152]{0:T(1024)(128)(4,1)S(1)}, s32[]{:S(2)}) async-start(s8[6291456]{0:T(1024)(128)(4,1)} %bitcast.615), calls=%async_computation.4 | async-start | bytes 4194304
  223.2 8.7 %slice-start.3 = ((s8[6291456]{0:T(1024)(128)(4,1)}), s8[4194304]{0:T(1024)(128)(4,1)S(1)}, s32[]{:S(2)}) async-start(s8[6291456]{0:T(1024)(128)(4,1)} %bitcast.615), calls=%async_computation.5 | async-start | bytes 8388608
  229.2 38.0 %copy-start.9 = (bf16[2,2,24,512]{3,2,1,0:T(8,128)(2,1)S(1)}, bf16[2,2,24,512]{3,2,1,0:T(8,128)(2,1)}, u32[]{:S(2)}) copy-start(bf16[2,2,24,512]{3,2,1,0:T(8,128)(2,1)} %param.12) | copy-start | bytes 294916
  271.5 5.0 %copy-start.11 = (s32[64]{0:T(128)S(1)}, s32[64]{0:T(128)}, u32[]{:S(2)}) copy-start(s32[64]{0:T(128)} %param.19) | copy-start | bytes 772
  272.0 7.7 %collective-permute-start.5 = (bf16[2,128,512]{2,1,0:T(8,128)(2,1)S(1)}, bf16[2,128,512]{2,1,0:T(8,128)(2,1)S(1)}, u32[]{:S(2)}, u32[]{:S(2)}) collective-permute-start(bf16[2,128,512]{2,1,0:T(8,128)(2,1)S(1)} %fusion.67), channel_id=1, source_target_pairs={{4,0},{8,4},{12,8},{16,12},{20,16},{24,20},{28,24},{0,28},{5,1},{9... | collective-permute-start | bytes 786440 | tf_op jit(solution)/shard_map/ppermute | solution.py:19
  275.4 9.1 %collective-permute-start.4 = (bf16[2,128,512]{2,1,0:T(8,128)(2,1)S(1)}, bf16[2,128,512]{2,1,0:T(8,128)(2,1)S(1)}, u32[]{:S(2)}, u32[]{:S(2)}) collective-permute-start(bf16[2,128,512]{2,1,0:T(8,128)(2,1)S(1)} %fusion.69), channel_id=1, source_target_pairs={{0,4},{4,8},{8,12},{12,16},{16,20},{20,24},{24,28},{28,0},{1,5},{5... | collective-permute-start | bytes 786440 | tf_op jit(solution)/shard_map/ppermute | solution.py:18
Sparse Core Ops, SparseCore 0:
  150.0 66.4 all-reduce.1
where the time goes:
time: 294 us; the launch traced here: 293 us
  blocking collectives  98.5 us (34%)
  waiting for transfers between devices  80.4 us (27%)
  matrix products  64.3 us (22%)
  starting transfers between devices  19.5 us (7%)
  between operations  15.3 us (5%)
  other arithmetic  8.67 us (3%)
  local copies, waits for them, and re-layouts  6.31 us (2%)
    psum x1, waiting for transfers between devices, per_device(): summed_focal = lax.psum(jnp.stack([focal_re, focal_im]), 'tile')  66.4 us
    dot_general x140, matrix products, plain_dot(): lax.dot_general(left, right, (((1,), (contract,)), ((), ())), preferred_e...  64.1 us
    all_gather x2, blocking collectives, per_device(): fold_shard_piece = lax.all_gather(coeff, 'tile', axis=2, tiled=True)  62 us
    all_gather x1, blocking collectives, apply_transpose(): shard_piece = lax.all_gather(projected, 'tile', axis=2, tiled=True)  30.7 us
    ppermute x3, starting transfers between devices, extended(): after = lax.ppermute(initial, axis, down)  13.3 us
    ppermute x3, waiting for transfers between devices, extended(): before = lax.ppermute(last, axis, up)  10.7 us
    all_to_all x1, starting transfers between devices, per_device(): lax.all_to_all(masked, 'tile', split_axis=1, concat_axis=2, tiled=True)  6 us
  transfers between devices with their start and end apart: 8, of which 5 were waited for; matrix products, arithmetic and copies ran while one was open for 13% of the time, Pallas kernels for 0%

commit v1 on v0

--- a/solution.py
+++ b/solution.py
@@ -105,7 +105,16 @@
         projected = jnp.stack(
             [jnp.concatenate(proj_re, axis=1), jnp.concatenate(proj_im, axis=1)]
         ).astype(jnp.bfloat16)
-        shard_piece = lax.all_gather(projected, "tile", axis=2, tiled=True)
+        degree = jax.lax.axis_size("tile")
+        earlier = [None] * degree
+        grid = [(ix, (ix + 1) % degree) for ix in range(degree)]
+        earlier[degree - 1] = projected
+        for u in range(degree - 2, -1, -1):
+            earlier[u] = jax.lax.ppermute(earlier[u + 1], "tile", grid)
+        now = jnp.concatenate(earlier, 2)
+        a_now = jax.lax.axis_index("tile")
+        arr_now = (a_now + 1) * projected.shape[2]
+        shard_piece = jnp.roll(now, shift=arr_now, axis=2)
         term_re, term_im = complex_dot(shard_piece[0], shard_piece[1], flipped[0], flipped[1], 1)
         summed_back = jnp.stack([term_re, term_im]).astype(jnp.bfloat16)
         far_re = []

time: 294 us -> 297 us (1.010)
  blocking collectives: 98.5 us -> 67.4 us
  waiting for transfers between devices: 80.4 us -> 111 us
  starting transfers between devices: 19.5 us -> 22.9 us
    ppermute x0 -> x7, waiting for transfers between devices: none -> 36.9 us  [apply_transpose(): earlier[u] = jax.lax.ppermute(earlier[u + 1], 'tile', grid)]
    all_gather x1 -> x0, blocking collectives: 30.7 us -> none  [apply_transpose(): shard_piece = lax.all_gather(projected, 'tile', axis=2, tiled=True)]
    ppermute x3, waiting for transfers between devices: 10.7 us -> 3.54 us  [extended(): before = lax.ppermute(last, axis, up)]
    psum x1, waiting for transfers between devices: 66.4 us -> 69.8 us  [per_device(): summed_focal = lax.psum(jnp.stack([focal_re, focal_im]), 'tile')]
  transfers between devices with their start and end apart: 8 -> 15, of which waited for: 5 -> 9; matrix products, arithmetic and copies ran while one was open for 13% -> 14% of each run, Pallas kernels for 0% -> 0%
where the time goes in v1:
time: 297 us; the launch traced here: 296 us
  waiting for transfers between devices  111 us (37%)
  blocking collectives  67.4 us (23%)
  matrix products  63.9 us (22%)
  starting transfers between devices  22.9 us (8%)
  between operations  15.4 us (5%)
  other arithmetic  8.78 us (3%)
  local copies, waits for them, and re-layouts  6.49 us (2%)
    psum x1, waiting for transfers between devices, per_device(): summed_focal = lax.psum(jnp.stack([focal_re, focal_im]), 'tile')  69.8 us
    dot_general x140, matrix products, plain_dot(): lax.dot_general(left, right, (((1,), (contract,)), ((), ())), preferred_e...  63.7 us
    all_gather x2, blocking collectives, per_device(): fold_shard_piece = lax.all_gather(coeff, 'tile', axis=2, tiled=True)  61.5 us
    ppermute x7, waiting for transfers between devices, apply_transpose(): earlier[u] = jax.lax.ppermute(earlier[u + 1], 'tile', grid)  36.9 us
    ppermute x3, starting transfers between devices, extended(): after = lax.ppermute(initial, axis, down)  10.8 us
    all_to_all x1, starting transfers between devices, per_device(): lax.all_to_all(masked, 'tile', split_axis=1, concat_axis=2, tiled=True)  7.31 us
  transfers between devices with their start and end apart: 15, of which 9 were waited for; matrix products, arithmetic and copies ran while one was open for 14% of the time, Pallas kernels for 0%

profile of v1, /device:TPU:0, one launch (start us, length us, event | category | flops | bytes accessed | tf_op | source)
XLA Modules:
  0.0 295.5 jit_solution(5066123522385099353)
XLA Ops:
  11.9 7.3 %all-to-all-start = ((bf16[8,2,2304]{2,1,0:T(2,128)(2,1)}), bf16[8,2,2304]{2,1,0:T(2,128)(2,1)S(1)}, u32[]{:S(2)}, u32[]{:S(2)}) async-start(bf16[8,2,2304]{2,1,0:T(2,128)(2,1)} %reshape.84), calls=%async_computation | async-start | bytes 147456 | tf_op jit(solution)/shard_map/all_to_all | solution.py:66
  19.2 2.0 fusion.463
  21.3 2.0 collective-permute-start
  23.2 2.8 collective-permute-start.1
  26.0 1.0 fusion.286
  27.0 1.1 fusion.272
  28.1 1.1 fusion.288
  29.1 1.1 fusion.274
  30.2 1.1 fusion.42
  31.3 1.1 fusion.43
  32.3 1.1 fusion.40
  33.4 1.1 fusion.41
  34.5 30.6 %all_gather.6 = bf16[2,128,384]{1,2,0:T(8,128)(2,1)S(1)} all-gather(bf16[2,128,48]{1,2,0:T(8,128)(2,1)S(1)} %pad_maximum_fusion.6), channel_id=1, replica_groups=mesh['tile'=8,'src'=4] {'tile'}, dimensions={2}, use_global_device_ids=true | all-gather | bytes 221184 | tf_op jit(solution)/shard_map/all_gather | solution.py:153
  68.4 1.3 fusion.148
  69.8 1.3 fusion.122
  71.1 1.3 fusion.94
  80.0 1.0 fusion.3
  83.3 1.2 copy.22
  84.5 1.8 fusion.175
  86.3 1.3 fusion.85
  87.6 1.5 fusion.20
  89.1 1.5 fusion.22
  90.7 1.3 fusion.167
  92.1 1.1 fusion.77
  93.2 1.1 fusion.23
  94.4 1.2 fusion.25
  97.1 30.9 %all_gather.7 = bf16[2,128,384]{1,2,0:T(8,128)(2,1)S(1)} all-gather(bf16[2,128,48]{1,2,0:T(8,128)(2,1)S(1)} %pad_maximum_fusion.7), channel_id=1, replica_groups=mesh['tile'=8,'src'=4] {'tile'}, dimensions={2}, use_global_device_ids=true | all-gather | bytes 221184 | tf_op jit(solution)/shard_map/all_gather | solution.py:153
  133.3 4.7 %collective-permute-start.3 = (bf16[2,128,512]{2,1,0:T(8,128)(2,1)S(1)}, bf16[2,128,512]{2,1,0:T(8,128)(2,1)S(1)}, u32[]{:S(2)}, u32[]{:S(2)}) collective-permute-start(bf16[2,128,512]{2,1,0:T(8,128)(2,1)S(1)} %get-tuple-element.10), channel_id=1, source_target_pairs={{4,0},{8,4},{12,8},{16,12},{20,16},{24,20},{28,24},{0,28},{5,1},{9... | collective-permute-start | bytes 786440 | tf_op jit(solution)/shard_map/ppermute | solution.py:19
  139.0 3.5 %collective-permute-done.2 = bf16[2,128,512]{2,1,0:T(8,128)(2,1)S(1)} collective-permute-done((bf16[2,128,512]{2,1,0:T(8,128)(2,1)S(1)}, bf16[2,128,512]{2,1,0:T(8,128)(2,1)S(1)}, u32[]{:S(2)}, u32[]{:S(2)}) %collective-permute-start.2) | collective-permute-done | bytes 262176 | tf_op jit(solution)/shard_map/ppermute | solution.py:18
  145.0 1.3 fusion.460
  148.1 69.8 %all-reduce.2.cloned.1.call-done = f32[2,128,64]{1,2,0:T(8,128)} async-done(((f32[2,128,64]{1,2,0:T(8,128)}), f32[2,128,64]{1,2,0:T(8,128)}) %all-reduce.2.cloned.1.call-update) | async-done | bytes 65552 | tf_op jit(solution)/shard_map/psum | solution.py:198
  218.8 5.8 %psum.15 = f32[64]{0:T(128)S(1)} all-reduce(f32[64]{0:T(128)S(1)} %add_reduce_fusion), channel_id=1, replica_groups=mesh['tile'=8,'src'=4] {'src'}, use_global_device_ids=true, to_apply=%region_2.3 | all-reduce | flops 64 | bytes 512 | tf_op jit(solution)/shard_map/psum | solution.py:199
  224.7 1.2 fusion.253
  225.9 1.1 fusion.259
  227.0 1.1 fusion
  228.1 1.1 fusion.1
  229.9 1.4 fusion.88
  231.3 1.3 fusion.80
  236.4 1.5 collective-permute-start.6
  241.8 3.3 %collective-permute-start.5 = (bf16[2,128,512]{2,1,0:T(8,128)(2,1)S(1)}, bf16[2,128,512]{2,1,0:T(8,128)(2,1)S(1)}, u32[]{:S(2)}, u32[]{:S(2)}) collective-permute-start(bf16[2,128,512]{2,1,0:T(8,128)(2,1)S(1)} %fusion.67), channel_id=1, source_target_pairs={{4,0},{8,4},{12,8},{16,12},{20,16},{24,20},{28,24},{0,28},{5,1},{9... | collective-permute-start | bytes 786440 | tf_op jit(solution)/shard_map/ppermute | solution.py:19
  245.2 6.5 %collective-permute-done.7 = bf16[2,128,48]{1,2,0:T(8,128)(2,1)S(1)} collective-permute-done((bf16[2,128,48]{1,2,0:T(8,128)(2,1)S(1)}, bf16[2,128,48]{1,2,0:T(8,128)(2,1)S(1)}, u32[]{:S(2)}, u32[]{:S(2)}) %collective-permute-start.7) | collective-permute-done | bytes 24608 | tf_op jit(solution)/shard_map/ppermute | solution.py:113
  251.7 1.1 collective-permute-start.8
  252.8 5.3 %collective-permute-done.8 = bf16[2,128,48]{1,2,0:T(8,128)(2,1)S(1)} collective-permute-done((bf16[2,128,48]{1,2,0:T(8,128)(2,1)S(1)}, bf16[2,128,48]{1,2,0:T(8,128)(2,1)S(1)}, u32[]{:S(2)}, u32[]{:S(2)}) %collective-permute-start.8) | collective-permute-done | bytes 24608 | tf_op jit(solution)/shard_map/ppermute | solution.py:113
  258.3 6.4 %collective-permute-done.9 = bf16[2,128,48]{1,2,0:T(8,128)(2,1)S(1)} collective-permute-done((bf16[2,128,48]{1,2,0:T(8,128)(2,1)S(1)}, bf16[2,128,48]{1,2,0:T(8,128)(2,1)S(1)}, u32[]{:S(2)}, u32[]{:S(2)}) %collective-permute-start.9) | collective-permute-done | bytes 24608 | tf_op jit(solution)/shard_map/ppermute | solution.py:113
  264.8 6.5 %collective-permute-done.10 = bf16[2,128,48]{1,2,0:T(8,128)(2,1)S(1)} collective-permute-done((bf16[2,128,48]{1,2,0:T(8,128)(2,1)S(1)}, bf16[2,128,48]{1,2,0:T(8,128)(2,1)S(1)}, u32[]{:S(2)}, u32[]{:S(2)}) %collective-permute-start.10) | collective-permute-done | bytes 24608 | tf_op jit(solution)/shard_map/ppermute | solution.py:113
  271.3 6.5 %collective-permute-done.11 = bf16[2,128,48]{1,2,0:T(8,128)(2,1)S(1)} collective-permute-done((bf16[2,128,48]{1,2,0:T(8,128)(2,1)S(1)}, bf16[2,128,48]{1,2,0:T(8,128)(2,1)S(1)}, u32[]{:S(2)}, u32[]{:S(2)}) %collective-permute-start.11) | collective-permute-done | bytes 24608 | tf_op jit(solution)/shard_map/ppermute | solution.py:113
  278.6 5.7 %collective-permute-done.12 = bf16[2,128,48]{1,2,0:T(8,128)(2,1)S(1)} collective-permute-done((bf16[2,128,48]{1,2,0:T(8,128)(2,1)S(1)}, bf16[2,128,48]{1,2,0:T(8,128)(2,1)S(1)}, u32[]{:S(2)}, u32[]{:S(2)}) %collective-permute-start.12) | collective-permute-done | bytes 24608 | tf_op jit(solution)/shard_map/ppermute | solution.py:113
  287.1 1.6 fusion.61
  (224 shorter events, 42.3 us)
Async XLA Ops:
  7.2 62.6 %copy-start.1 = (bf16[2,128,1024]{2,1,0:T(8,128)(2,1)S(1)}, bf16[2,128,1024]{2,1,0:T(8,128)(2,1)}, u32[]{:S(2)}) copy-start(bf16[2,128,1024]{2,1,0:T(8,128)(2,1)} %param.10) | copy-start | bytes 1572868
  9.8 63.8 %copy-start.2 = (bf16[2,2,24,512]{3,2,1,0:T(8,128)(2,1)S(1)}, bf16[2,2,24,512]{3,2,1,0:T(8,128)(2,1)}, u32[]{:S(2)}) copy-start(bf16[2,2,24,512]{3,2,1,0:T(8,128)(2,1)} %param.13) | copy-start | bytes 294916
  11.9 70.5 %all-to-all-start = ((bf16[8,2,2304]{2,1,0:T(2,128)(2,1)}), bf16[8,2,2304]{2,1,0:T(2,128)(2,1)S(1)}, u32[]{:S(2)}, u32[]{:S(2)}) async-start(bf16[8,2,2304]{2,1,0:T(2,128)(2,1)} %reshape.84), calls=%async_computation | async-start | bytes 147456 | tf_op jit(solution)/shard_map/all_to_all | solution.py:66
  19.2 198.8 %all-reduce.2.cloned.1.call-start = ((), (), s32[]{:S(2)}) async-start(), calls=%async_computation.1 | async-start | bytes 131072 | tf_op jit(solution)/shard_map/psum | solution.py:198
  19.2 53.1 %copy-start = (bf16[2,3,2,512,512]{4,3,2,1,0:T(8,128)(2,1)S(1)}, bf16[2,3,2,512,512]{4,3,2,1,0:T(8,128)(2,1)}, u32[]{:S(2)}) copy-start(bf16[2,3,2,512,512]{4,3,2,1,0:T(8,128)(2,1)} %param.11) | copy-start | bytes 18874372
  21.3 63.2 %collective-permute-start = (bf16[2,128,512]{2,1,0:T(8,128)(2,1)}, bf16[2,128,512]{2,1,0:T(8,128)(2,1)}, u32[]{:S(2)}, u32[]{:S(2)}) collective-permute-start(bf16[2,128,512]{2,1,0:T(8,128)(2,1)} %get-tuple-element.11), channel_id=1, source_target_pairs={{0,4},{4,8},{8,12},{12,16},{16,20},{20,24},{24,28},{28,0},{1,5},{5... | collective-permute-start | bytes 786440 | tf_op jit(solution)/shard_map/ppermute | solution.py:18
  23.2 63.0 %collective-permute-start.1 = (bf16[2,128,512]{2,1,0:T(8,128)(2,1)}, bf16[2,128,512]{2,1,0:T(8,128)(2,1)}, u32[]{:S(2)}, u32[]{:S(2)}) collective-permute-start(bf16[2,128,512]{2,1,0:T(8,128)(2,1)} %get-tuple-element.12), channel_id=1, source_target_pairs={{4,0},{8,4},{12,8},{16,12},{20,16},{24,20},{28,24},{0,28},{5,1},{9... | collective-permute-start | bytes 786440 | tf_op jit(solution)/shard_map/ppermute | solution.py:19
  77.9 14.2 %slice-start = ((s8[6291456]{0:T(1024)(128)(4,1)}), s8[2097152]{0:T(1024)(128)(4,1)S(1)}, s32[]{:S(2)}) async-start(s8[6291456]{0:T(1024)(128)(4,1)} %bitcast.613), calls=%async_computation.2 | async-start | bytes 4194304
  83.3 9.9 %copy-start.6 = (f32[128,512]{1,0:T(8,128)S(1)}, f32[128,512]{1,0:T(8,128)}, u32[]{:S(2)}) copy-start(f32[128,512]{1,0:T(8,128)} %convolution_subtract_fusion.23) | copy-start | bytes 786436
  83.3 9.9 %copy-start.7 = (f32[128,512]{1,0:T(8,128)S(1)}, f32[128,512]{1,0:T(8,128)}, u32[]{:S(2)}) copy-start(f32[128,512]{1,0:T(8,128)} %fusion.3) | copy-start | bytes 786436
  83.3 11.1 %copy-start.4 = (f32[128,512]{1,0:T(8,128)S(1)}, f32[128,512]{1,0:T(8,128)}, u32[]{:S(2)}) copy-start(f32[128,512]{1,0:T(8,128)} %convolution_subtract_fusion.16) | copy-start | bytes 786436
  83.3 11.1 %copy-start.5 = (f32[128,512]{1,0:T(8,128)S(1)}, f32[128,512]{1,0:T(8,128)}, u32[]{:S(2)}) copy-start(f32[128,512]{1,0:T(8,128)} %convolution_subtract_fusion.17) | copy-start | bytes 786436
  83.3 8.8 %slice-start.1 = ((s8[6291456]{0:T(1024)(128)(4,1)}), s8[4194304]{0:T(1024)(128)(4,1)S(1)}, s32[]{:S(2)}) async-start(s8[6291456]{0:T(1024)(128)(4,1)} %bitcast.613), calls=%async_computation.3 | async-start | bytes 8388608
  87.6 8.2 %copy-start.8 = (bf16[2,2,24,512]{3,2,1,0:T(8,128)(2,1)S(1)}, bf16[2,2,24,512]{3,2,1,0:T(8,128)(2,1)}, u32[]{:S(2)}) copy-start(bf16[2,2,24,512]{3,2,1,0:T(8,128)(2,1)} %param.12) | copy-start | bytes 294916
  133.3 9.2 %collective-permute-start.2 = (bf16[2,128,512]{2,1,0:T(8,128)(2,1)S(1)}, bf16[2,128,512]{2,1,0:T(8,128)(2,1)S(1)}, u32[]{:S(2)}, u32[]{:S(2)}) collective-permute-start(bf16[2,128,512]{2,1,0:T(8,128)(2,1)S(1)} %get-tuple-element.9), channel_id=1, source_target_pairs={{0,4},{4,8},{8,12},{12,16},{16,20},{20,24},{24,28},{28,0},{1,5},{5... | collective-permute-start | bytes 786440 | tf_op jit(solution)/shard_map/ppermute | solution.py:18
  133.3 9.8 %collective-permute-start.3 = (bf16[2,128,512]{2,1,0:T(8,128)(2,1)S(1)}, bf16[2,128,512]{2,1,0:T(8,128)(2,1)S(1)}, u32[]{:S(2)}, u32[]{:S(2)}) collective-permute-start(bf16[2,128,512]{2,1,0:T(8,128)(2,1)S(1)} %get-tuple-element.10), channel_id=1, source_target_pairs={{4,0},{8,4},{12,8},{16,12},{20,16},{24,20},{28,24},{0,28},{5,1},{9... | collective-permute-start | bytes 786440 | tf_op jit(solution)/shard_map/ppermute | solution.py:19
  143.9 2.4 copy-start.3
  144.1 80.5 %copy-start.10 = (f32[64]{0:T(128)S(1)}, f32[64]{0:T(128)}, u32[]{:S(2)}) copy-start(f32[64]{0:T(128)} %param.18) | copy-start | bytes 772
  145.0 87.7 %slice-start.2 = ((s8[6291456]{0:T(1024)(128)(4,1)}), s8[2097152]{0:T(1024)(128)(4,1)S(1)}, s32[]{:S(2)}) async-start(s8[6291456]{0:T(1024)(128)(4,1)} %bitcast.615), calls=%async_computation.4 | async-start | bytes 4194304
  224.7 8.0 %slice-start.3 = ((s8[6291456]{0:T(1024)(128)(4,1)}), s8[4194304]{0:T(1024)(128)(4,1)S(1)}, s32[]{:S(2)}) async-start(s8[6291456]{0:T(1024)(128)(4,1)} %bitcast.615), calls=%async_computation.5 | async-start | bytes 8388608
  236.4 8.7 %collective-permute-start.6 = (bf16[2,128,48]{1,2,0:T(8,128)(2,1)S(1)}, bf16[2,128,48]{1,2,0:T(8,128)(2,1)S(1)}, u32[]{:S(2)}, u32[]{:S(2)}) collective-permute-start(bf16[2,128,48]{1,2,0:T(8,128)(2,1)S(1)} %pad_maximum_fusion.8), channel_id=1, source_target_pairs={{0,4},{4,8},{8,12},{12,16},{16,20},{20,24},{24,28},{28,0},{1,5},{5... | collective-permute-start | bytes 73736 | tf_op jit(solution)/shard_map/ppermute | solution.py:113
  240.7 37.0 %copy-start.11 = (s32[64]{0:T(128)S(1)}, s32[64]{0:T(128)}, u32[]{:S(2)}) copy-start(s32[64]{0:T(128)} %param.19) | copy-start | bytes 772
  241.1 43.9 %copy-start.9 = (bf16[2,2,24,512]{3,2,1,0:T(8,128)(2,1)S(1)}, bf16[2,2,24,512]{3,2,1,0:T(8,128)(2,1)}, u32[]{:S(2)}) copy-start(bf16[2,2,24,512]{3,2,1,0:T(8,128)(2,1)} %param.12) | copy-start | bytes 294916
  241.8 45.2 %collective-permute-start.5 = (bf16[2,128,512]{2,1,0:T(8,128)(2,1)S(1)}, bf16[2,128,512]{2,1,0:T(8,128)(2,1)S(1)}, u32[]{:S(2)}, u32[]{:S(2)}) collective-permute-start(bf16[2,128,512]{2,1,0:T(8,128)(2,1)S(1)} %fusion.67), channel_id=1, source_target_pairs={{4,0},{8,4},{12,8},{16,12},{20,16},{24,20},{28,24},{0,28},{5,1},{9... | collective-permute-start | bytes 786440 | tf_op jit(solution)/shard_map/ppermute | solution.py:19
  245.1 6.5 %collective-permute-start.7 = (bf16[2,128,48]{1,2,0:T(8,128)(2,1)S(1)}, bf16[2,128,48]{1,2,0:T(8,128)(2,1)S(1)}, u32[]{:S(2)}, u32[]{:S(2)}) collective-permute-start(bf16[2,128,48]{1,2,0:T(8,128)(2,1)S(1)} %collective-permute-done.6), channel_id=1, source_target_pairs={{0,4},{4,8},{8,12},{12,16},{16,20},{20,24},{24,28},{28,0},{1,5},{5... | collective-permute-start | bytes 73736 | tf_op jit(solution)/shard_map/ppermute | solution.py:113
  251.7 6.5 %collective-permute-start.8 = (bf16[2,128,48]{1,2,0:T(8,128)(2,1)S(1)}, bf16[2,128,48]{1,2,0:T(8,128)(2,1)S(1)}, u32[]{:S(2)}, u32[]{:S(2)}) collective-permute-start(bf16[2,128,48]{1,2,0:T(8,128)(2,1)S(1)} %collective-permute-done.7), channel_id=1, source_target_pairs={{0,4},{4,8},{8,12},{12,16},{16,20},{20,24},{24,28},{28,0},{1,5},{5... | collective-permute-start | bytes 73736 | tf_op jit(solution)/shard_map/ppermute | solution.py:113
  258.2 6.5 %collective-permute-start.9 = (bf16[2,128,48]{1,2,0:T(8,128)(2,1)S(1)}, bf16[2,128,48]{1,2,0:T(8,128)(2,1)S(1)}, u32[]{:S(2)}, u32[]{:S(2)}) collective-permute-start(bf16[2,128,48]{1,2,0:T(8,128)(2,1)S(1)} %collective-permute-done.8), channel_id=1, source_target_pairs={{0,4},{4,8},{8,12},{12,16},{16,20},{20,24},{24,28},{28,0},{1,5},{5... | collective-permute-start | bytes 73736 | tf_op jit(solution)/shard_map/ppermute | solution.py:113
  258.2 28.8 %collective-permute-start.4 = (bf16[2,128,512]{2,1,0:T(8,128)(2,1)S(1)}, bf16[2,128,512]{2,1,0:T(8,128)(2,1)S(1)}, u32[]{:S(2)}, u32[]{:S(2)}) collective-permute-start(bf16[2,128,512]{2,1,0:T(8,128)(2,1)S(1)} %fusion.69), channel_id=1, source_target_pairs={{0,4},{4,8},{8,12},{12,16},{16,20},{20,24},{24,28},{28,0},{1,5},{5... | collective-permute-start | bytes 786440 | tf_op jit(solution)/shard_map/ppermute | solution.py:18
  264.7 6.5 %collective-permute-start.10 = (bf16[2,128,48]{1,2,0:T(8,128)(2,1)S(1)}, bf16[2,128,48]{1,2,0:T(8,128)(2,1)S(1)}, u32[]{:S(2)}, u32[]{:S(2)}) collective-permute-start(bf16[2,128,48]{1,2,0:T(8,128)(2,1)S(1)} %collective-permute-done.9), channel_id=1, source_target_pairs={{0,4},{4,8},{8,12},{12,16},{16,20},{20,24},{24,28},{28,0},{1,5},{5... | collective-permute-start | bytes 73736 | tf_op jit(solution)/shard_map/ppermute | solution.py:113
  271.2 6.5 %collective-permute-start.11 = (bf16[2,128,48]{1,2,0:T(8,128)(2,1)S(1)}, bf16[2,128,48]{1,2,0:T(8,128)(2,1)S(1)}, u32[]{:S(2)}, u32[]{:S(2)}) collective-permute-start(bf16[2,128,48]{1,2,0:T(8,128)(2,1)S(1)} %collective-permute-done.10), channel_id=1, source_target_pairs={{0,4},{4,8},{8,12},{12,16},{16,20},{20,24},{24,28},{28,0},{1,5},{5... | collective-permute-start | bytes 73736 | tf_op jit(solution)/shard_map/ppermute | solution.py:113
  277.8 6.5 %collective-permute-start.12 = (bf16[2,128,48]{1,2,0:T(8,128)(2,1)S(1)}, bf16[2,128,48]{1,2,0:T(8,128)(2,1)S(1)}, u32[]{:S(2)}, u32[]{:S(2)}) collective-permute-start(bf16[2,128,48]{1,2,0:T(8,128)(2,1)S(1)} %collective-permute-done.11), channel_id=1, source_target_pairs={{0,4},{4,8},{8,12},{12,16},{16,20},{20,24},{24,28},{28,0},{1,5},{5... | collective-permute-start | bytes 73736 | tf_op jit(solution)/shard_map/ppermute | solution.py:113
Sparse Core Ops, SparseCore 0:
  147.9 69.9 all-reduce.1
